TPU v7x, 32 devices: a whole 2x2x4 slice. The times are simulated.
32 devices in a mesh: groups: 2 (over x), expert: 16 (over z, y, core).
Axes of the slice: x: 2, y: 2, z: 4, core: 2. Of those that a mesh axis runs over, the one named last changes fastest.
Arguments:
- hidden_in: bfloat16 [256, 4096], P(('groups', 'expert')), parts along dimension 0, may hold values from -6 to 6
- queries: bfloat16 [256, 4096], P(('groups', 'expert')), parts along dimension 0, may hold values from -8 to 8
- decode_key_value: bfloat16 [256, 2, 256], P(('groups', 'expert')), parts along dimension 0, may hold values from -6 to 6
- local_kv: bfloat16 [1024, 2, 16, 256], P(('groups', 'expert')), parts along dimension 0, may hold values from -8 to 8
- page_table: int32 [256, 16], P(('groups', 'expert')), parts along dimension 0, may hold values from 0 to 31
- seq_blocks: int32 [256], P(('groups', 'expert')), parts along dimension 0, may hold values from 1 to 16
- prompt_kv: bfloat16 [32, 16, 2, 16, 256], P(('groups', 'expert')), parts along dimension 0, may hold values from -8 to 8
- prompt_owner: int32 [32], P('groups'), parts along dimension 0, may hold values from 0 to 15, as said below
- prompt_pages: int32 [32], P('groups'), parts along dimension 0, may hold values from 1 to 16
- norm_gain: float32 [4096], replicated, may hold values from 0.5 to 1.5
- router: bfloat16 [4096, 8], replicated, may hold values from -0.09375 to 0.09375
- w_gate: bfloat16 [16, 4096, 384], P('expert'), may hold values from -0.09375 to 0.09375
- w_up: bfloat16 [16, 4096, 384], P('expert'), may hold values from -0.09375 to 0.09375
- w_down: bfloat16 [16, 384, 4096], P('expert'), may hold values from -0.21875 to 0.21875
- route_ids: int32 [256, 8], P(('groups', 'expert')), parts along dimension 0, may hold values from 0 to 7, as said below
Outputs:
- layer_out: bfloat16 [256, 4096], P(('groups', 'expert')), parts along dimension 0
There are 2 independent parts, one for each index of `groups`. A program takes and returns all parts, laid end to end along the dimension named above; an argument that names none is the same for every part. Nothing has to cross between parts.
Inputs may be any that keep to these rules, and one draw needn't show every extreme that they name: `prompt_owner`: each device is named by at most 2 prompts, and by exactly 2 for some of the devices. `route_ids`: each row names 8 different experts; among the rows of one device no expert is named more than 8 times, a bound that some block reaches. `page_table`: indices among the pages of the sequence's own device.
All inputs are finite; a program needn't handle non-finite values.
Results may differ from a plain program's by a relative error of at most 0.0056.
Values may be sent and summed in bfloat16 or wider, within the bound.
No kernel may reach another device: no remote copies, remote signals or barrier semaphores. Data moves between devices by JAX's collectives and lax.ppermute only.
A program may use at most 128 MiB of HBM per device.

v0:
```python
import math
import jax
import jax.numpy as jnp
from jax import lax
from jax.sharding import PartitionSpec as P

D = 4096
QUERY_HEADS = 32
KEY_VALUE_HEADS = 2
HEAD_SIZE = 128
PAGE_TOKENS = 16
TOPK = 8
MAXB = 16
MAXP = 2
norm_eps = 1e-06
masked_score = -1e30


def partner(x, axis, apart):
    return lax.ppermute(x, axis, [(i, i ^ 1 << apart) for i in range(lax.axis_size(axis))])


def attend(rows_of_queries, rows_of_keys, rows_of_values, allowed, token_own_key, token_own_value):
    decode_tokens = rows_of_queries.shape[0]
    heads_of_queries = rows_of_queries.reshape(
        decode_tokens, KEY_VALUE_HEADS, QUERY_HEADS // KEY_VALUE_HEADS, HEAD_SIZE
    )
    heads_of_keys = rows_of_keys.reshape(decode_tokens, -1, KEY_VALUE_HEADS, HEAD_SIZE)
    heads_of_values = rows_of_values.reshape(decode_tokens, -1, KEY_VALUE_HEADS, HEAD_SIZE)
    scale_for_scores = 1.0 / math.sqrt(HEAD_SIZE)
    allowed_mask = allowed[:, None, None, :]
    scores = (
        jnp.einsum(
            "tkgd,tlkd->tkgl", heads_of_queries, heads_of_keys, preferred_element_type=jnp.float32
        )
        * scale_for_scores
    )
    scores = jnp.where(allowed_mask, scores, masked_score)
    token_own_score = (
        jnp.einsum(
            "xejp,xep->xej",
            heads_of_queries,
            token_own_key.reshape(decode_tokens, KEY_VALUE_HEADS, HEAD_SIZE),
            preferred_element_type=jnp.float32,
        )
        * scale_for_scores
    )
    peak = jnp.maximum(jnp.max(scores, -1), token_own_score)
    weights = jnp.where(allowed_mask, jnp.exp(scores - peak[..., None]), 0.0)
    own_weight = jnp.exp(token_own_score - peak)
    denominator = jnp.sum(weights, -1) + own_weight
    probs = (weights / denominator[..., None]).astype(jnp.bfloat16)
    token_own_probability = (own_weight / denominator).astype(jnp.bfloat16)
    blended_noise = jnp.einsum(
        "tkgl,tlkd->tkgd", probs, heads_of_values, preferred_element_type=jnp.float32
    )
    blended_noise = blended_noise + token_own_probability.astype(jnp.float32)[
        ..., None
    ] * token_own_value.reshape(decode_tokens, KEY_VALUE_HEADS, 1, HEAD_SIZE).astype(jnp.float32)
    return blended_noise.reshape(decode_tokens, QUERY_HEADS * HEAD_SIZE).astype(jnp.bfloat16)


def all_tokens(resid_wide, normed, spread, w_gate, w_up, w_down):
    devices = lax.axis_size("expert")
    seq_dev, experts = spread.shape
    expert = lax.axis_index("expert") // 2
    bits = devices.bit_length() - 1
    coarse = lax.reduce_precision(spread, 8, 7)
    fine = spread - coarse
    pad = -2 * experts % 128
    tail = jnp.pad(jnp.concatenate([coarse, fine], 1), ((0, 0), (0, pad))).astype(jnp.bfloat16)
    rows = jnp.concatenate([normed, tail], 1)
    for bit in reversed(range(bits)):
        rows = jnp.concatenate([rows, partner(rows, "expert", bit)], 0)
    gates = rows[:, D : D + 2 * experts].astype(jnp.float32).reshape(-1, 2, experts)
    own = jnp.arange(experts, dtype=jnp.int32) == expert
    gate = jnp.sum(jnp.where(own, gates, 0.0), (1, 2))
    tokens = rows[:, :D]
    gate_proj = jnp.dot(tokens, w_gate, preferred_element_type=jnp.float32)
    up_proj = jnp.dot(tokens, w_up, preferred_element_type=jnp.float32)
    activated = (jax.nn.silu(gate_proj) * up_proj).astype(jnp.bfloat16)
    mixed = jnp.dot(activated, w_down, preferred_element_type=jnp.float32) * gate[:, None]
    for bit in range(bits):
        half = mixed.shape[0] // 2
        moved = partner(mixed[half:].astype(jnp.bfloat16), "expert", bit)
        mixed = mixed[:half] + moved.astype(jnp.float32)
    return (resid_wide + mixed).astype(jnp.bfloat16)


def local(
    hidden_in,
    queries,
    decode_key_value,
    local_kv,
    page_table,
    seq_blocks,
    prompt_kv,
    prompt_owner,
    prompt_pages,
    norm_gain,
    router,
    w_gate,
    w_up,
    w_down,
    route_ids,
):
    devices = lax.axis_size("expert")
    position = lax.axis_index("expert")
    experts = devices // 2
    seq_dev = hidden_in.shape[0]
    key_value_width = KEY_VALUE_HEADS * HEAD_SIZE
    capacity = min(seq_dev, max(2, 2 * ((3 * seq_dev * TOPK + 2 * devices - 1) // (2 * devices))))
    half_cap = capacity // 2
    even_core = position % 2 == 0
    prompt_count = prompt_owner.shape[0]
    prompt_range = jnp.arange(prompt_count, dtype=jnp.int32)
    same_owner = prompt_owner[:, None] == prompt_owner[None, :]
    earlier = prompt_range[None, :] < prompt_range[:, None]
    arrival = jnp.sum((same_owner & earlier).astype(jnp.int32), 1)
    matching = (
        prompt_owner[None, None, :] == jnp.arange(devices, dtype=jnp.int32)[:, None, None]
    ) & (arrival[None, None, :] == jnp.arange(MAXP, dtype=jnp.int32)[None, :, None])
    chosen_prompt = jnp.sum(jnp.where(matching, prompt_range[None, None, :], 0), -1)
    occupied = jnp.any(matching, -1)
    own_picks = lax.dynamic_index_in_dim(chosen_prompt, position, 0, keepdims=False)
    own_occupied = lax.dynamic_index_in_dim(occupied, position, 0, keepdims=False)
    page_rows = prompt_kv[0]
    outgoing = jnp.take(page_rows, chosen_prompt.T.reshape(-1), axis=0).reshape(
        MAXP, devices, 2, PAGE_TOKENS, key_value_width
    )
    outgoing = jnp.where(occupied.T[:, :, None, None, None], outgoing, 0)
    arrived = lax.all_to_all(outgoing, "expert", split_axis=1, concat_axis=1, tiled=True)
    lengths = jnp.take(prompt_pages, own_picks)
    new_keys = arrived[:, :, 0].reshape(MAXP, devices * PAGE_TOKENS, key_value_width)
    new_values = arrived[:, :, 1].reshape(MAXP, devices * PAGE_TOKENS, key_value_width)
    new_allowed = (jnp.arange(devices * PAGE_TOKENS, dtype=jnp.int32) // PAGE_TOKENS)[
        None, :
    ] < lengths[:, None]
    fresh_rows = attend(
        queries[:MAXP],
        new_keys,
        new_values,
        new_allowed,
        decode_key_value[:MAXP, 0],
        decode_key_value[:MAXP, 1],
    )
    fetched = local_kv[page_table]
    old_keys = fetched[:, :, 0].reshape(seq_dev, MAXB * PAGE_TOKENS, key_value_width)
    old_values = fetched[:, :, 1].reshape(seq_dev, MAXB * PAGE_TOKENS, key_value_width)
    old_allowed = (jnp.arange(MAXB * PAGE_TOKENS, dtype=jnp.int32) // PAGE_TOKENS)[
        None, :
    ] < seq_blocks[:, None]
    old_out = attend(
        queries, old_keys, old_values, old_allowed, decode_key_value[:, 0], decode_key_value[:, 1]
    )
    new_count = jnp.sum(own_occupied.astype(jnp.int32))
    is_new = jnp.arange(MAXP, dtype=jnp.int32) < new_count
    attention = jnp.concatenate(
        [jnp.where(is_new[:, None], fresh_rows, old_out[:MAXP]), old_out[MAXP:]], 0
    )
    residual = (hidden_in.astype(jnp.float32) + attention.astype(jnp.float32)).astype(jnp.bfloat16)
    resid_wide = residual.astype(jnp.float32)
    normed = (
        resid_wide
        * lax.rsqrt(jnp.mean(resid_wide * resid_wide, -1, keepdims=True) + norm_eps)
        * norm_gain
    ).astype(jnp.bfloat16)
    logits = jnp.dot(normed, router, preferred_element_type=jnp.float32)
    expert_onehot = route_ids[:, :, None] == jnp.arange(experts, dtype=jnp.int32)[None, None, :]
    selected = jnp.sum(jnp.where(expert_onehot, logits[:, None, :], 0.0), -1)
    gate_weights = jax.nn.softmax(selected, -1)
    if capacity >= seq_dev and devices & devices - 1 == 0:
        spread = jnp.sum(jnp.where(expert_onehot, gate_weights[:, :, None], 0.0), 1)
        return all_tokens(resid_wide, normed, spread, w_gate[0], w_up[0], w_down[0])
    assigned = seq_dev * TOPK
    expert_ids = route_ids.reshape(assigned)
    chosen = (expert_ids[:, None] == jnp.arange(experts, dtype=jnp.int32)[None, :]).astype(
        jnp.int32
    )
    before = jnp.cumsum(chosen, 0) - chosen
    slot_rank = jnp.sum(before * chosen, 1)
    slot_index = expert_ids * capacity + slot_rank
    placing = slot_index[None, :] == jnp.arange(experts * capacity, dtype=jnp.int32)[:, None]
    selector = jnp.any(placing.reshape(experts * capacity, seq_dev, TOPK), -1).astype(jnp.bfloat16)
    gathered_rows = jnp.dot(selector, normed, preferred_element_type=jnp.float32).astype(
        jnp.bfloat16
    )
    outgoing_half = gathered_rows.reshape(devices, half_cap, D)
    own_half = lax.all_to_all(outgoing_half, "expert", split_axis=0, concat_axis=0, tiled=True)
    partner_half = partner(own_half, "expert", 0)
    received = jnp.where(
        even_core,
        jnp.concatenate([own_half, partner_half], 1),
        jnp.concatenate([partner_half, own_half], 1),
    )
    flattened = received.reshape(devices * capacity, D)
    gate_proj = jnp.dot(flattened, w_gate[0], preferred_element_type=jnp.float32)
    up_proj = jnp.dot(flattened, w_up[0], preferred_element_type=jnp.float32)
    activated = (jax.nn.silu(gate_proj) * up_proj).astype(jnp.bfloat16)
    partial_value = jnp.dot(activated, w_down[0], preferred_element_type=jnp.float32).reshape(
        devices, capacity, D
    )
    kept = jnp.where(even_core, partial_value[:, :half_cap], partial_value[:, half_cap:])
    handed = jnp.where(even_core, partial_value[:, half_cap:], partial_value[:, :half_cap])
    partner_part = partner(handed, "expert", 0)
    finished = (kept + partner_part).astype(jnp.bfloat16)
    returned = lax.all_to_all(finished, "expert", split_axis=0, concat_axis=0, tiled=True)
    expert_sum = returned.reshape(experts * capacity, D)
    picked = jnp.take(expert_sum, slot_index, axis=0).astype(jnp.float32).reshape(seq_dev, TOPK, D)
    expert_mix = jnp.sum(picked * gate_weights[:, :, None], 1)
    return (resid_wide + expert_mix).astype(jnp.bfloat16)


def solution(mesh):
    return jax.shard_map(
        local,
        mesh=mesh,
        in_specs=(
            P(("groups", "expert"), None),
            P(("groups", "expert"), None),
            P(("groups", "expert"), None, None),
            P(("groups", "expert"), None, None, None),
            P(("groups", "expert"), None),
            P(("groups", "expert")),
            P(("groups", "expert"), None, None, None, None),
            P("groups"),
            P("groups"),
            P(),
            P(),
            P("expert", None, None),
            P("expert", None, None),
            P("expert", None, None),
            P(("groups", "expert"), None),
        ),
        out_specs=P(("groups", "expert"), None),
        check_vma=False,
    )
```

profile of v0, /device:TPU:0, one launch (start us, length us, event | category | flops | bytes accessed | tf_op | source)
XLA Modules:
  0.0 98.2 jit_solution(18162269884148207099)
XLA Ops:
  2.8 2.3 %gather_fusion.1 = bf16[32,2,16,256]{3,2,1,0:T(8,128)(2,1)} fusion(bf16[16,2,16,256]{3,2,1,0:T(8,128)(2,1)} %bitcast.87, s32[1024]{0:T(1024)S(1)} %get-tuple-element.26), kind=kCustom, calls=%fused_computation.1 | custom fusion | bytes 1048704 | tf_op jit(solution)/shard_map/jit(_take)/gather | solution.py:128
  7.2 7.5 %all-to-all-start = ((bf16[2,16,2,16,256]{4,3,0,2,1:T(8,128)(2,1)}), bf16[2,16,2,16,256]{4,3,0,2,1:T(8,128)(2,1)}, u32[]{:S(2)}, u32[]{:S(2)}) async-start(bf16[2,16,2,16,256]{4,3,0,2,1:T(8,128)(2,1)} %copy.48), calls=%async_computation | async-start | bytes 1048576 | tf_op jit(solution)/shard_map/all_to_all | solution.py:132
  14.7 3.1 %gather_fusion.2 = bf16[128,2,16,256]{3,2,1,0:T(8,128)(2,1)} fusion(bf16[32,2,16,256]{3,2,1,0:T(8,128)(2,1)} %param.18, s32[1024]{0:T(1024)S(1)} %get-tuple-element.25), kind=kCustom, calls=%fused_computation.2 | custom fusion | bytes 4194816 | tf_op jit(solution)/shard_map/gather | solution.py:147
  17.8 3.0 %slice_bitcast_fusion.1 = (bf16[8,16,1,16,256]{4,3,1,0,2:T(8,128)(2,1)}, bf16[8,16,1,16,256]{4,3,1,0,2:T(8,128)(2,1)}) fusion(bf16[8,16,2,16,256]{4,3,2,1,0:T(8,128)(2,1)} %bitcast.85), kind=kLoop, calls=%fused_computation.22 | loop fusion | bytes 4194304
  20.8 2.2 %reshape_reshape_squeeze.15 = bf16[8,256,2,128]{3,2,1,0:T(2,128)(2,1)} reshape(bf16[8,16,1,16,256]{4,3,1,0,2:T(8,128)(2,1)} %get-tuple-element.8) | data formatting | bytes 2097152 | tf_op jit(solution)/shard_map/reshape;reshape;squeeze | solution.py:29
  23.0 2.2 %reshape_reshape_squeeze.14 = bf16[8,256,2,128]{3,2,1,0:T(2,128)(2,1)} reshape(bf16[8,16,1,16,256]{4,3,1,0,2:T(8,128)(2,1)} %get-tuple-element.7) | data formatting | bytes 2097152 | tf_op jit(solution)/shard_map/reshape;reshape;squeeze | solution.py:28
  25.5 1.8 %fusion.66 = (f32[8,2,16]{2,1,0:T(2,128)S(1)}, f32[8,2,16,256]{3,2,1,0:T(8,128)S(1)}) fusion(bf16[8,2,16,128]{3,0,2,1:T(8,128)(2,1)S(1)} %bitcast.103, bf16[8,256,2,128]{3,2,1,0:T(2,128)(2,1)} %reshape_reshape_squeeze.14, pred[8,256]{1,0:T(8,128)(4,1)S(1)} %broadcast_compare_fusion), kind=kOutput, calls=%fused_computation.142 | convolution fusion | flops 16973568 | bytes 1379328 | tf_op jit(solution)/shard_map/tkgd,tlkd->tkgl/dot_general | solution.py:33
  32.4 1.8 %fusion.65 = (bf16[2,16,1,16,256]{4,3,0,2,1:T(8,128)(2,1)}, bf16[2,16,1,16,256]{4,3,0,2,1:T(8,128)(2,1)S(1)}) fusion(bf16[2,16,2,16,256]{4,3,0,2,1:T(8,128)(2,1)} %all-to-all-done), kind=kLoop, calls=%fused_computation.141 | loop fusion | bytes 1048576 | tf_op jit(solution)/shard_map/slice | solution.py:134
  43.9 2.8 %collective-permute-start = (bf16[8,4224]{1,0:T(8,128)(2,1)S(1)}, bf16[8,4224]{1,0:T(8,128)(2,1)S(1)}, u32[]{:S(2)}, u32[]{:S(2)}) collective-permute-start(bf16[8,4224]{1,0:T(8,128)(2,1)S(1)} %get-tuple-element.11), channel_id=1, source_target_pairs={{0,8},{1,9},{2,10},{3,11},{4,12},{5,13},{6,14},{7,15},{8,0},{9,1},... | collective-permute-start | bytes 202760 | tf_op jit(solution)/shard_map/ppermute | solution.py:20
  46.8 3.9 %collective-permute-done = bf16[8,4224]{1,0:T(8,128)(2,1)S(1)} collective-permute-done((bf16[8,4224]{1,0:T(8,128)(2,1)S(1)}, bf16[8,4224]{1,0:T(8,128)(2,1)S(1)}, u32[]{:S(2)}, u32[]{:S(2)}) %collective-permute-start) | collective-permute-done | bytes 67616 | tf_op jit(solution)/shard_map/ppermute | solution.py:20
  52.0 3.8 %collective-permute-done.1 = bf16[16,4224]{1,0:T(8,128)(2,1)S(1)} collective-permute-done((bf16[16,4224]{1,0:T(8,128)(2,1)S(1)}, bf16[16,4224]{1,0:T(8,128)(2,1)S(1)}, u32[]{:S(2)}, u32[]{:S(2)}) %collective-permute-start.1) | collective-permute-done | bytes 135200 | tf_op jit(solution)/shard_map/ppermute | solution.py:20
  55.8 1.8 %collective-permute-start.2 = (bf16[32,4224]{1,0:T(8,128)(2,1)S(1)}, bf16[32,4224]{1,0:T(8,128)(2,1)S(1)}, u32[]{:S(2)}, u32[]{:S(2)}) collective-permute-start(bf16[32,4224]{1,0:T(8,128)(2,1)S(1)} %pad_maximum_fusion.1), channel_id=1, source_target_pairs={{0,2},{1,3},{2,0},{3,1},{4,6},{5,7},{6,4},{7,5},{8,10},{9,11},{10,... | collective-permute-start | bytes 811016 | tf_op jit(solution)/shard_map/ppermute | solution.py:20
  58.3 4.0 %collective-permute-done.2 = bf16[32,4224]{1,0:T(8,128)(2,1)S(1)} collective-permute-done((bf16[32,4224]{1,0:T(8,128)(2,1)S(1)}, bf16[32,4224]{1,0:T(8,128)(2,1)S(1)}, u32[]{:S(2)}, u32[]{:S(2)}) %collective-permute-start.2) | collective-permute-done | bytes 270368 | tf_op jit(solution)/shard_map/ppermute | solution.py:20
  66.1 1.9 %fusion.1 = f32[128,384]{1,0:T(8,128)S(1)} fusion(bf16[1,4096,384]{2,1,0:T(8,128)(2,1)S(1)} %copy-done.2, bf16[128,4224]{1,0:T(8,128)(2,1)} %constant_dynamic-update-slice_fusion), kind=kOutput, calls=%fused_computation.5 | convolution fusion | flops 402653184 | bytes 4390912 | tf_op jit(solution)/shard_map/dot_general | solution.py:80
  68.0 5.0 %convolution_multiply_fusion = f32[128,4096]{1,0:T(8,128)} fusion(bf16[1,384,4096]{2,1,0:T(8,128)(2,1)S(1)} %copy-done, f32[128]{0:T(128)S(1)} %select_reduce_fusion, f32[128,384]{1,0:T(8,128)S(1)} %fusion.1, bf16[1,4096,384]{2,1,0:T(8,128)(2,1)} %param.26, bf16[128,4224]{1,0:T(8,128)(2,1)} %constant_dynamic-update-slice_fusion), kind=kOutput, calls=%fused_computation.3 | convolution fusion | flops 806125568 | bytes 9634304 | tf_op jit(solution)/shard_map/dot_general | solution.py:82
  73.0 1.3 %slice.146 = bf16[64,4096]{1,0:T(8,128)(2,1)S(1)} slice(f32[128,4096]{1,0:T(8,128)} %convolution_multiply_fusion), slice={[64:128], [0:4096]} | slice | bytes 1048576 | tf_op jit(solution)/shard_map/slice | solution.py:85
  74.5 1.8 %collective-permute-done.4 = bf16[64,4096]{1,0:T(8,128)(2,1)S(1)} collective-permute-done((bf16[64,4096]{1,0:T(8,128)(2,1)S(1)}, bf16[64,4096]{1,0:T(8,128)(2,1)S(1)}, u32[]{:S(2)}, u32[]{:S(2)}) %collective-permute-start.4) | collective-permute-done | bytes 524320 | tf_op jit(solution)/shard_map/ppermute | solution.py:20
  76.3 1.3 %slice_add_fusion = f32[64,4096]{1,0:T(8,128)S(1)} fusion(f32[128,4096]{1,0:T(8,128)} %convolution_multiply_fusion, bf16[64,4096]{1,0:T(8,128)(2,1)S(1)} %collective-permute-done.4), kind=kLoop, calls=%fused_computation.20 | loop fusion | flops 524288 | bytes 2621440 | tf_op jit(solution)/shard_map/add | solution.py:86
  77.6 1.8 %collective-permute-start.5 = (bf16[32,4096]{1,0:T(8,128)(2,1)S(1)}, bf16[32,4096]{1,0:T(8,128)(2,1)S(1)}, u32[]{:S(2)}, u32[]{:S(2)}) collective-permute-start(bf16[32,4096]{1,0:T(8,128)(2,1)S(1)} %slice.147), channel_id=1, source_target_pairs={{0,2},{1,3},{2,0},{3,1},{4,6},{5,7},{6,4},{7,5},{8,10},{9,11},{10,... | collective-permute-start | bytes 786440 | tf_op jit(solution)/shard_map/ppermute | solution.py:20
  79.4 6.6 %collective-permute-done.5 = bf16[32,4096]{1,0:T(8,128)(2,1)S(1)} collective-permute-done((bf16[32,4096]{1,0:T(8,128)(2,1)S(1)}, bf16[32,4096]{1,0:T(8,128)(2,1)S(1)}, u32[]{:S(2)}, u32[]{:S(2)}) %collective-permute-start.5) | collective-permute-done | bytes 262176 | tf_op jit(solution)/shard_map/ppermute | solution.py:20
  86.1 2.2 %collective-permute-start.6 = (bf16[16,4096]{1,0:T(8,128)(2,1)S(1)}, bf16[16,4096]{1,0:T(8,128)(2,1)S(1)}, u32[]{:S(2)}, u32[]{:S(2)}) collective-permute-start(bf16[16,4096]{1,0:T(8,128)(2,1)S(1)} %slice.148), channel_id=1, source_target_pairs={{0,4},{1,5},{2,6},{3,7},{4,0},{5,1},{6,2},{7,3},{8,12},{9,13},{10,... | collective-permute-start | bytes 393224 | tf_op jit(solution)/shard_map/ppermute | solution.py:20
  88.3 2.9 %collective-permute-done.6 = bf16[16,4096]{1,0:T(8,128)(2,1)S(1)} collective-permute-done((bf16[16,4096]{1,0:T(8,128)(2,1)S(1)}, bf16[16,4096]{1,0:T(8,128)(2,1)S(1)}, u32[]{:S(2)}, u32[]{:S(2)}) %collective-permute-start.6) | collective-permute-done | bytes 131104 | tf_op jit(solution)/shard_map/ppermute | solution.py:20
  91.3 4.0 %collective-permute-start.7 = (bf16[8,4096]{1,0:T(8,128)(2,1)S(1)}, bf16[8,4096]{1,0:T(8,128)(2,1)S(1)}, u32[]{:S(2)}, u32[]{:S(2)}) collective-permute-start(bf16[8,4096]{1,0:T(8,128)(2,1)S(1)} %slice.149), channel_id=1, source_target_pairs={{0,8},{1,9},{2,10},{3,11},{4,12},{5,13},{6,14},{7,15},{8,0},{9,1},... | collective-permute-start | bytes 196616 | tf_op jit(solution)/shard_map/ppermute | solution.py:20
  95.3 2.2 %collective-permute-done.7 = bf16[8,4096]{1,0:T(8,128)(2,1)S(1)} collective-permute-done((bf16[8,4096]{1,0:T(8,128)(2,1)S(1)}, bf16[8,4096]{1,0:T(8,128)(2,1)S(1)}, u32[]{:S(2)}, u32[]{:S(2)}) %collective-permute-start.7) | collective-permute-done | bytes 65568 | tf_op jit(solution)/shard_map/ppermute | solution.py:20
  (109 shorter events, 26.7 us)
Async XLA Ops:
  0.0 68.0 %copy-start = (bf16[1,384,4096]{2,1,0:T(8,128)(2,1)S(1)}, bf16[1,384,4096]{2,1,0:T(8,128)(2,1)}, u32[]{:S(2)}) copy-start(bf16[1,384,4096]{2,1,0:T(8,128)(2,1)} %param.28) | copy-start | bytes 9437188
  7.2 25.2 %all-to-all-start = ((bf16[2,16,2,16,256]{4,3,0,2,1:T(8,128)(2,1)}), bf16[2,16,2,16,256]{4,3,0,2,1:T(8,128)(2,1)}, u32[]{:S(2)}, u32[]{:S(2)}) async-start(bf16[2,16,2,16,256]{4,3,0,2,1:T(8,128)(2,1)} %copy.48), calls=%async_computation | async-start | bytes 1048576 | tf_op jit(solution)/shard_map/all_to_all | solution.py:132
  23.0 2.2 %copy-start.7 = (bf16[8,2,256]{2,1,0:T(2,128)(2,1)S(1)}, bf16[8,2,256]{2,1,0:T(2,128)(2,1)}, u32[]{:S(2)}) copy-start(bf16[8,2,256]{2,1,0:T(2,128)(2,1)} %param.17) | copy-start | bytes 24580
  23.0 2.3 %copy-start.13 = (s32[8]{0:T(128)S(1)}, s32[8]{0:T(128)}, u32[]{:S(2)}) copy-start(s32[8]{0:T(128)} %param.20) | copy-start | bytes 100
  23.0 2.4 %copy-start.11 = (bf16[8,4096]{1,0:T(8,128)(2,1)S(1)}, bf16[8,4096]{1,0:T(8,128)(2,1)}, u32[]{:S(2)}) copy-start(bf16[8,4096]{1,0:T(8,128)(2,1)} %param.16) | copy-start | bytes 196612
  25.5 2.1 %copy-start.3 = (bf16[8,256,2,128]{3,2,1,0:T(2,128)(2,1)S(1)}, bf16[8,256,2,128]{3,2,1,0:T(2,128)(2,1)}, u32[]{:S(2)}) copy-start(bf16[8,256,2,128]{3,2,1,0:T(2,128)(2,1)} %reshape_reshape_squeeze.15) | copy-start | bytes 3145732
  27.5 1.2 %copy-start.1 = (s32[16]{0:T(128)S(1)}, s32[16]{0:T(128)}, u32[]{:S(2)}) copy-start(s32[16]{0:T(128)} %param.23) | copy-start | bytes 196
  27.9 6.3 %copy-start.4 = (bf16[8,2,16,128]{3,2,1,0:T(8,128)(2,1)}, bf16[8,2,16,128]{3,2,1,0:T(8,128)(2,1)S(1)}, u32[]{:S(2)}) copy-start(bf16[8,2,16,128]{3,2,1,0:T(8,128)(2,1)S(1)} %fusion.7) | copy-start | bytes 196612
  28.7 5.4 %copy-start.10 = (bf16[1,2,32,128]{3,2,1,0:T(8,128)(2,1)}, bf16[1,2,32,128]{3,2,1,0:T(8,128)(2,1)S(1)}, u32[]{:S(2)}) copy-start(bf16[1,2,32,128]{3,2,1,0:T(8,128)(2,1)S(1)} %copy.66) | copy-start | bytes 49156
  34.9 6.4 %slice-start = ((bf16[8,2,16,128]{3,2,1,0:T(8,128)(2,1)}), bf16[2,2,16,128]{3,2,1,0:T(8,128)(2,1)S(1)}, s32[]{:S(2)}) async-start(bf16[8,2,16,128]{3,2,1,0:T(8,128)(2,1)} %copy-done.4), calls=%async_computation.1 | async-start | bytes 32768 | tf_op jit(solution)/shard_map/slice | solution.py:159
  34.9 6.5 %copy-start.5 = (bf16[8,4096]{1,0:T(8,128)(2,1)S(1)}, bf16[8,4096]{1,0:T(8,128)(2,1)}, u32[]{:S(2)}) copy-start(bf16[8,4096]{1,0:T(8,128)(2,1)} %param.15) | copy-start | bytes 196612
  36.7 4.6 %copy-start.12 = (pred[2]{0:T(512)(128)(4,1)S(1)}, pred[2]{0:T(512)(128)(4,1)}, u32[]{:S(2)}) copy-start(pred[2]{0:T(512)(128)(4,1)} %iota_compare_fusion.6) | copy-start | bytes 10
  36.7 4.9 %copy-start.8 = (f32[4096]{0:T(1024)S(1)}, f32[4096]{0:T(1024)}, u32[]{:S(2)}) copy-start(f32[4096]{0:T(1024)} %param.24) | copy-start | bytes 49156
  36.7 5.0 %copy-start.6 = (bf16[4096,8]{0,1:T(8,128)(2,1)S(1)}, bf16[4096,8]{0,1:T(8,128)(2,1)}, u32[]{:S(2)}) copy-start(bf16[4096,8]{0,1:T(8,128)(2,1)} %param.25) | copy-start | bytes 196612
  36.7 5.2 %copy-start.9 = (s32[8,8]{1,0:T(8,128)S(1)}, s32[8,8]{1,0:T(8,128)}, u32[]{:S(2)}) copy-start(s32[8,8]{1,0:T(8,128)} %param.29) | copy-start | bytes 772
  43.9 6.7 %collective-permute-start = (bf16[8,4224]{1,0:T(8,128)(2,1)S(1)}, bf16[8,4224]{1,0:T(8,128)(2,1)S(1)}, u32[]{:S(2)}, u32[]{:S(2)}) collective-permute-start(bf16[8,4224]{1,0:T(8,128)(2,1)S(1)} %get-tuple-element.11), channel_id=1, source_target_pairs={{0,8},{1,9},{2,10},{3,11},{4,12},{5,13},{6,14},{7,15},{8,0},{9,1},... | collective-permute-start | bytes 202760 | tf_op jit(solution)/shard_map/ppermute | solution.py:20
  50.7 5.1 %collective-permute-start.1 = (bf16[16,4224]{1,0:T(8,128)(2,1)S(1)}, bf16[16,4224]{1,0:T(8,128)(2,1)S(1)}, u32[]{:S(2)}, u32[]{:S(2)}) collective-permute-start(bf16[16,4224]{1,0:T(8,128)(2,1)S(1)} %pad_maximum_fusion.2), channel_id=1, source_target_pairs={{0,4},{1,5},{2,6},{3,7},{4,0},{5,1},{6,2},{7,3},{8,12},{9,13},{10,... | collective-permute-start | bytes 405512 | tf_op jit(solution)/shard_map/ppermute | solution.py:20
  55.8 10.3 %copy-start.2 = (bf16[1,4096,384]{2,1,0:T(8,128)(2,1)S(1)}, bf16[1,4096,384]{2,1,0:T(8,128)(2,1)}, u32[]{:S(2)}) copy-start(bf16[1,4096,384]{2,1,0:T(8,128)(2,1)} %param.27) | copy-start | bytes 9437188
  55.8 6.5 %collective-permute-start.2 = (bf16[32,4224]{1,0:T(8,128)(2,1)S(1)}, bf16[32,4224]{1,0:T(8,128)(2,1)S(1)}, u32[]{:S(2)}, u32[]{:S(2)}) collective-permute-start(bf16[32,4224]{1,0:T(8,128)(2,1)S(1)} %pad_maximum_fusion.1), channel_id=1, source_target_pairs={{0,2},{1,3},{2,0},{3,1},{4,6},{5,7},{6,4},{7,5},{8,10},{9,11},{10,... | collective-permute-start | bytes 811016 | tf_op jit(solution)/shard_map/ppermute | solution.py:20
  62.4 2.0 %collective-permute-start.3 = (bf16[64,4224]{1,0:T(8,128)(2,1)S(1)}, bf16[64,4224]{1,0:T(8,128)(2,1)S(1)}, u32[]{:S(2)}, u32[]{:S(2)}) collective-permute-start(bf16[64,4224]{1,0:T(8,128)(2,1)S(1)} %pad_maximum_fusion), channel_id=1, source_target_pairs={{0,1},{1,0},{2,3},{3,2},{4,5},{5,4},{6,7},{7,6},{8,9},{9,8},{10,11... | collective-permute-start | bytes 1622024 | tf_op jit(solution)/shard_map/ppermute | solution.py:20
  74.3 2.0 %collective-permute-start.4 = (bf16[64,4096]{1,0:T(8,128)(2,1)S(1)}, bf16[64,4096]{1,0:T(8,128)(2,1)S(1)}, u32[]{:S(2)}, u32[]{:S(2)}) collective-permute-start(bf16[64,4096]{1,0:T(8,128)(2,1)S(1)} %slice.146), channel_id=1, source_target_pairs={{0,1},{1,0},{2,3},{3,2},{4,5},{5,4},{6,7},{7,6},{8,9},{9,8},{10,11... | collective-permute-start | bytes 1572872 | tf_op jit(solution)/shard_map/ppermute | solution.py:20
  77.6 8.4 %collective-permute-start.5 = (bf16[32,4096]{1,0:T(8,128)(2,1)S(1)}, bf16[32,4096]{1,0:T(8,128)(2,1)S(1)}, u32[]{:S(2)}, u32[]{:S(2)}) collective-permute-start(bf16[32,4096]{1,0:T(8,128)(2,1)S(1)} %slice.147), channel_id=1, source_target_pairs={{0,2},{1,3},{2,0},{3,1},{4,6},{5,7},{6,4},{7,5},{8,10},{9,11},{10,... | collective-permute-start | bytes 786440 | tf_op jit(solution)/shard_map/ppermute | solution.py:20
  86.1 5.1 %collective-permute-start.6 = (bf16[16,4096]{1,0:T(8,128)(2,1)S(1)}, bf16[16,4096]{1,0:T(8,128)(2,1)S(1)}, u32[]{:S(2)}, u32[]{:S(2)}) collective-permute-start(bf16[16,4096]{1,0:T(8,128)(2,1)S(1)} %slice.148), channel_id=1, source_target_pairs={{0,4},{1,5},{2,6},{3,7},{4,0},{5,1},{6,2},{7,3},{8,12},{9,13},{10,... | collective-permute-start | bytes 393224 | tf_op jit(solution)/shard_map/ppermute | solution.py:20
  91.3 6.2 %collective-permute-start.7 = (bf16[8,4096]{1,0:T(8,128)(2,1)S(1)}, bf16[8,4096]{1,0:T(8,128)(2,1)S(1)}, u32[]{:S(2)}, u32[]{:S(2)}) collective-permute-start(bf16[8,4096]{1,0:T(8,128)(2,1)S(1)} %slice.149), channel_id=1, source_target_pairs={{0,8},{1,9},{2,10},{3,11},{4,12},{5,13},{6,14},{7,15},{8,0},{9,1},... | collective-permute-start | bytes 196616 | tf_op jit(solution)/shard_map/ppermute | solution.py:20
where the time goes:
time: 99.1 us; the launch traced here: 98.2 us
  waiting for transfers between devices  26.4 us (27%)
  local copies, waits for them, and re-layouts  23.2 us (23%)
  starting transfers between devices  21 us (21%)
  other arithmetic  14.7 us (15%)
  matrix products  12.4 us (13%)
    ppermute x8, waiting for transfers between devices, partner(): lax.ppermute(x, axis, [(i, i ^ 1 << apart) for i in range(lax.axis_size(a...  26.4 us
    ppermute x8, starting transfers between devices, partner(): lax.ppermute(x, axis, [(i, i ^ 1 << apart) for i in range(lax.axis_size(a...  13.6 us
    all_to_all x1, starting transfers between devices, local(): lax.all_to_all(outgoing, 'expert', split_axis=1, concat_axis=1, tiled=True)  7.46 us
    unnamed x36, local copies, waits for them, and re-layouts  5.18 us
    dot_general x1, matrix products, all_tokens(): jnp.dot(activated, w_down, preferred_element_type=jnp.float32)  4.98 us
    gather x1, local copies, waits for them, and re-layouts, local(): fetched = local_kv[page_table]  3.07 us
    dot_general x2, matrix products, attend(): jnp.einsum('tkgd,tlkd->tkgl', heads_of_queries, heads_of_keys, preferred_...  3.04 us
    another operation x2, local copies, waits for them, and re-layouts, attend(): rows_of_keys.reshape(decode_tokens, -1, KEY_VALUE_HEADS, HEAD_SIZE)  3 us
  transfers between devices with their start and end apart: 9, of which 8 were waited for; matrix products, arithmetic and copies ran while one was open for 20% of the time, Pallas kernels for 0%

commit v1 on v0

--- a/solution.py
+++ b/solution.py
@@ -129,7 +129,12 @@
         MAXP, devices, 2, PAGE_TOKENS, key_value_width
     )
     outgoing = jnp.where(occupied.T[:, :, None, None, None], outgoing, 0)
-    arrived = lax.all_to_all(outgoing, "expert", split_axis=1, concat_axis=1, tiled=True)
+    arrived = jnp.concatenate(
+        lax.all_to_all(
+            jnp.stack(jnp.split(outgoing, lax.axis_size("expert"), axis=1)), "expert", 0, 0
+        ),
+        axis=1,
+    )
     lengths = jnp.take(prompt_pages, own_picks)
     new_keys = arrived[:, :, 0].reshape(MAXP, devices * PAGE_TOKENS, key_value_width)
     new_values = arrived[:, :, 1].reshape(MAXP, devices * PAGE_TOKENS, key_value_width)

time: 99.1 us -> 99.3 us (level)
    unnamed x36 -> x51, local copies, waits for them, and re-layouts: 5.18 us -> 5.25 us
where the time goes in v1:
time: 99.3 us; the launch traced here: 98.4 us
  waiting for transfers between devices  26.4 us (27%)
  local copies, waits for them, and re-layouts  23.3 us (23%)
  starting transfers between devices  21 us (21%)
  other arithmetic  14.7 us (15%)
  matrix products  12.4 us (12%)
    ppermute x8, waiting for transfers between devices, partner(): lax.ppermute(x, axis, [(i, i ^ 1 << apart) for i in range(lax.axis_size(a...  26.4 us
    ppermute x8, starting transfers between devices, partner(): lax.ppermute(x, axis, [(i, i ^ 1 << apart) for i in range(lax.axis_size(a...  13.6 us
    all_to_all x1, starting transfers between devices, local(): lax.all_to_all(jnp.stack(jnp.split(outgoing, lax.axis_size('expert'), axi...  7.46 us
    unnamed x51, local copies, waits for them, and re-layouts  5.25 us
    dot_general x1, matrix products, all_tokens(): jnp.dot(activated, w_down, preferred_element_type=jnp.float32)  4.98 us
    gather x1, local copies, waits for them, and re-layouts, local(): fetched = local_kv[page_table]  3.07 us
    dot_general x2, matrix products, attend(): jnp.einsum('tkgd,tlkd->tkgl', heads_of_queries, heads_of_keys, preferred_...  3.04 us
    another operation x2, local copies, waits for them, and re-layouts, attend(): rows_of_keys.reshape(decode_tokens, -1, KEY_VALUE_HEADS, HEAD_SIZE)  3 us
  transfers between devices with their start and end apart: 9, of which 8 were waited for; matrix products, arithmetic and copies ran while one was open for 20% of the time, Pallas kernels for 0%

profile of v1, /device:TPU:0, one launch (start us, length us, event | category | flops | bytes accessed | tf_op | source)
XLA Modules:
  0.0 98.4 jit_solution(491363810281834953)
XLA Ops:
  2.8 2.3 %gather_fusion.1 = bf16[32,2,16,256]{3,2,1,0:T(8,128)(2,1)} fusion(bf16[16,2,16,256]{3,2,1,0:T(8,128)(2,1)} %bitcast.184, s32[1024]{0:T(1024)S(1)} %get-tuple-element.26), kind=kCustom, calls=%fused_computation.1 | custom fusion | bytes 1048704 | tf_op jit(solution)/shard_map/jit(_take)/gather | solution.py:128
  7.4 7.5 %all-to-all-start = ((bf16[16,2,1,2,16,256]{5,4,1,3,2,0:T(8,128)(2,1)}), bf16[16,2,1,2,16,256]{5,4,1,3,2,0:T(8,128)(2,1)}, u32[]{:S(2)}, u32[]{:S(2)}) async-start(bf16[16,2,1,2,16,256]{5,4,1,3,2,0:T(8,128)(2,1)} %copy.109), calls=%async_computation | async-start | bytes 1048576 | tf_op jit(solution)/shard_map/all_to_all | solution.py:133
  14.9 3.1 %gather_fusion.2 = bf16[128,2,16,256]{3,2,1,0:T(8,128)(2,1)} fusion(bf16[32,2,16,256]{3,2,1,0:T(8,128)(2,1)} %param.18, s32[1024]{0:T(1024)S(1)} %get-tuple-element.25), kind=kCustom, calls=%fused_computation.2 | custom fusion | bytes 4194816 | tf_op jit(solution)/shard_map/gather | solution.py:152
  17.9 3.0 %slice_bitcast_fusion.1 = (bf16[8,16,1,16,256]{4,3,1,0,2:T(8,128)(2,1)}, bf16[8,16,1,16,256]{4,3,1,0,2:T(8,128)(2,1)}) fusion(bf16[8,16,2,16,256]{4,3,2,1,0:T(8,128)(2,1)} %bitcast.182), kind=kLoop, calls=%fused_computation.22 | loop fusion | bytes 4194304
  21.0 2.2 %reshape_reshape_squeeze.15 = bf16[8,256,2,128]{3,2,1,0:T(2,128)(2,1)} reshape(bf16[8,16,1,16,256]{4,3,1,0,2:T(8,128)(2,1)} %get-tuple-element.8) | data formatting | bytes 2097152 | tf_op jit(solution)/shard_map/reshape;reshape;squeeze | solution.py:29
  23.2 2.2 %reshape_reshape_squeeze.14 = bf16[8,256,2,128]{3,2,1,0:T(2,128)(2,1)} reshape(bf16[8,16,1,16,256]{4,3,1,0,2:T(8,128)(2,1)} %get-tuple-element.7) | data formatting | bytes 2097152 | tf_op jit(solution)/shard_map/reshape;reshape;squeeze | solution.py:28
  25.7 1.8 %fusion.66 = (f32[8,2,16]{2,1,0:T(2,128)S(1)}, f32[8,2,16,256]{3,2,1,0:T(8,128)S(1)}) fusion(bf16[8,2,16,128]{3,0,2,1:T(8,128)(2,1)S(1)} %bitcast.200, bf16[8,256,2,128]{3,2,1,0:T(2,128)(2,1)} %reshape_reshape_squeeze.14, pred[8,256]{1,0:T(8,128)(4,1)S(1)} %broadcast_compare_fusion), kind=kOutput, calls=%fused_computation.174 | convolution fusion | flops 16973568 | bytes 1379328 | tf_op jit(solution)/shard_map/tkgd,tlkd->tkgl/dot_general | solution.py:33
  32.5 1.8 %fusion.65 = (bf16[2,16,1,16,256]{4,3,0,2,1:T(8,128)(2,1)}, bf16[2,16,1,16,256]{4,3,0,2,1:T(8,128)(2,1)S(1)}) fusion(bf16[2,16,2,16,256]{4,3,0,2,1:T(8,128)(2,1)} %bitcast.23), kind=kLoop, calls=%fused_computation.173 | loop fusion | bytes 1048576 | tf_op jit(solution)/shard_map/slice | solution.py:139
  44.1 2.8 %collective-permute-start = (bf16[8,4224]{1,0:T(8,128)(2,1)S(1)}, bf16[8,4224]{1,0:T(8,128)(2,1)S(1)}, u32[]{:S(2)}, u32[]{:S(2)}) collective-permute-start(bf16[8,4224]{1,0:T(8,128)(2,1)S(1)} %get-tuple-element.11), channel_id=1, source_target_pairs={{0,8},{1,9},{2,10},{3,11},{4,12},{5,13},{6,14},{7,15},{8,0},{9,1},... | collective-permute-start | bytes 202760 | tf_op jit(solution)/shard_map/ppermute | solution.py:20
  47.0 3.9 %collective-permute-done = bf16[8,4224]{1,0:T(8,128)(2,1)S(1)} collective-permute-done((bf16[8,4224]{1,0:T(8,128)(2,1)S(1)}, bf16[8,4224]{1,0:T(8,128)(2,1)S(1)}, u32[]{:S(2)}, u32[]{:S(2)}) %collective-permute-start) | collective-permute-done | bytes 67616 | tf_op jit(solution)/shard_map/ppermute | solution.py:20
  52.2 3.8 %collective-permute-done.1 = bf16[16,4224]{1,0:T(8,128)(2,1)S(1)} collective-permute-done((bf16[16,4224]{1,0:T(8,128)(2,1)S(1)}, bf16[16,4224]{1,0:T(8,128)(2,1)S(1)}, u32[]{:S(2)}, u32[]{:S(2)}) %collective-permute-start.1) | collective-permute-done | bytes 135200 | tf_op jit(solution)/shard_map/ppermute | solution.py:20
  56.0 1.8 %collective-permute-start.2 = (bf16[32,4224]{1,0:T(8,128)(2,1)S(1)}, bf16[32,4224]{1,0:T(8,128)(2,1)S(1)}, u32[]{:S(2)}, u32[]{:S(2)}) collective-permute-start(bf16[32,4224]{1,0:T(8,128)(2,1)S(1)} %pad_maximum_fusion.1), channel_id=1, source_target_pairs={{0,2},{1,3},{2,0},{3,1},{4,6},{5,7},{6,4},{7,5},{8,10},{9,11},{10,... | collective-permute-start | bytes 811016 | tf_op jit(solution)/shard_map/ppermute | solution.py:20
  58.5 4.0 %collective-permute-done.2 = bf16[32,4224]{1,0:T(8,128)(2,1)S(1)} collective-permute-done((bf16[32,4224]{1,0:T(8,128)(2,1)S(1)}, bf16[32,4224]{1,0:T(8,128)(2,1)S(1)}, u32[]{:S(2)}, u32[]{:S(2)}) %collective-permute-start.2) | collective-permute-done | bytes 270368 | tf_op jit(solution)/shard_map/ppermute | solution.py:20
  66.3 1.9 %fusion.1 = f32[128,384]{1,0:T(8,128)S(1)} fusion(bf16[1,4096,384]{2,1,0:T(8,128)(2,1)S(1)} %copy-done.2, bf16[128,4224]{1,0:T(8,128)(2,1)} %constant_dynamic-update-slice_fusion.16), kind=kOutput, calls=%fused_computation.5 | convolution fusion | flops 402653184 | bytes 4390912 | tf_op jit(solution)/shard_map/dot_general | solution.py:80
  68.2 5.0 %convolution_multiply_fusion = f32[128,4096]{1,0:T(8,128)} fusion(bf16[1,384,4096]{2,1,0:T(8,128)(2,1)S(1)} %copy-done, f32[128]{0:T(128)S(1)} %select_reduce_fusion, f32[128,384]{1,0:T(8,128)S(1)} %fusion.1, bf16[1,4096,384]{2,1,0:T(8,128)(2,1)} %param.26, bf16[128,4224]{1,0:T(8,128)(2,1)} %constant_dynamic-update-slice_fusion.16), kind=kOutput, calls=%fused_computation.3 | convolution fusion | flops 806125568 | bytes 9634304 | tf_op jit(solution)/shard_map/dot_general | solution.py:82
  73.2 1.3 %slice.146 = bf16[64,4096]{1,0:T(8,128)(2,1)S(1)} slice(f32[128,4096]{1,0:T(8,128)} %convolution_multiply_fusion), slice={[64:128], [0:4096]} | slice | bytes 1048576 | tf_op jit(solution)/shard_map/slice | solution.py:85
  74.7 1.8 %collective-permute-done.4 = bf16[64,4096]{1,0:T(8,128)(2,1)S(1)} collective-permute-done((bf16[64,4096]{1,0:T(8,128)(2,1)S(1)}, bf16[64,4096]{1,0:T(8,128)(2,1)S(1)}, u32[]{:S(2)}, u32[]{:S(2)}) %collective-permute-start.4) | collective-permute-done | bytes 524320 | tf_op jit(solution)/shard_map/ppermute | solution.py:20
  76.5 1.3 %slice_add_fusion = f32[64,4096]{1,0:T(8,128)S(1)} fusion(f32[128,4096]{1,0:T(8,128)} %convolution_multiply_fusion, bf16[64,4096]{1,0:T(8,128)(2,1)S(1)} %collective-permute-done.4), kind=kLoop, calls=%fused_computation.20 | loop fusion | flops 524288 | bytes 2621440 | tf_op jit(solution)/shard_map/add | solution.py:86
  77.8 1.8 %collective-permute-start.5 = (bf16[32,4096]{1,0:T(8,128)(2,1)S(1)}, bf16[32,4096]{1,0:T(8,128)(2,1)S(1)}, u32[]{:S(2)}, u32[]{:S(2)}) collective-permute-start(bf16[32,4096]{1,0:T(8,128)(2,1)S(1)} %slice.147), channel_id=1, source_target_pairs={{0,2},{1,3},{2,0},{3,1},{4,6},{5,7},{6,4},{7,5},{8,10},{9,11},{10,... | collective-permute-start | bytes 786440 | tf_op jit(solution)/shard_map/ppermute | solution.py:20
  79.6 6.6 %collective-permute-done.5 = bf16[32,4096]{1,0:T(8,128)(2,1)S(1)} collective-permute-done((bf16[32,4096]{1,0:T(8,128)(2,1)S(1)}, bf16[32,4096]{1,0:T(8,128)(2,1)S(1)}, u32[]{:S(2)}, u32[]{:S(2)}) %collective-permute-start.5) | collective-permute-done | bytes 262176 | tf_op jit(solution)/shard_map/ppermute | solution.py:20
  86.3 2.2 %collective-permute-start.6 = (bf16[16,4096]{1,0:T(8,128)(2,1)S(1)}, bf16[16,4096]{1,0:T(8,128)(2,1)S(1)}, u32[]{:S(2)}, u32[]{:S(2)}) collective-permute-start(bf16[16,4096]{1,0:T(8,128)(2,1)S(1)} %slice.148), channel_id=1, source_target_pairs={{0,4},{1,5},{2,6},{3,7},{4,0},{5,1},{6,2},{7,3},{8,12},{9,13},{10,... | collective-permute-start | bytes 393224 | tf_op jit(solution)/shard_map/ppermute | solution.py:20
  88.5 2.9 %collective-permute-done.6 = bf16[16,4096]{1,0:T(8,128)(2,1)S(1)} collective-permute-done((bf16[16,4096]{1,0:T(8,128)(2,1)S(1)}, bf16[16,4096]{1,0:T(8,128)(2,1)S(1)}, u32[]{:S(2)}, u32[]{:S(2)}) %collective-permute-start.6) | collective-permute-done | bytes 131104 | tf_op jit(solution)/shard_map/ppermute | solution.py:20
  91.5 4.0 %collective-permute-start.7 = (bf16[8,4096]{1,0:T(8,128)(2,1)S(1)}, bf16[8,4096]{1,0:T(8,128)(2,1)S(1)}, u32[]{:S(2)}, u32[]{:S(2)}) collective-permute-start(bf16[8,4096]{1,0:T(8,128)(2,1)S(1)} %slice.149), channel_id=1, source_target_pairs={{0,8},{1,9},{2,10},{3,11},{4,12},{5,13},{6,14},{7,15},{8,0},{9,1},... | collective-permute-start | bytes 196616 | tf_op jit(solution)/shard_map/ppermute | solution.py:20
  95.5 2.2 %collective-permute-done.7 = bf16[8,4096]{1,0:T(8,128)(2,1)S(1)} collective-permute-done((bf16[8,4096]{1,0:T(8,128)(2,1)S(1)}, bf16[8,4096]{1,0:T(8,128)(2,1)S(1)}, u32[]{:S(2)}, u32[]{:S(2)}) %collective-permute-start.7) | collective-permute-done | bytes 65568 | tf_op jit(solution)/shard_map/ppermute | solution.py:20
  (125 shorter events, 26.7 us)
Async XLA Ops:
  0.0 68.2 %copy-start = (bf16[1,384,4096]{2,1,0:T(8,128)(2,1)S(1)}, bf16[1,384,4096]{2,1,0:T(8,128)(2,1)}, u32[]{:S(2)}) copy-start(bf16[1,384,4096]{2,1,0:T(8,128)(2,1)} %param.28) | copy-start | bytes 9437188
  7.4 25.2 %all-to-all-start = ((bf16[16,2,1,2,16,256]{5,4,1,3,2,0:T(8,128)(2,1)}), bf16[16,2,1,2,16,256]{5,4,1,3,2,0:T(8,128)(2,1)}, u32[]{:S(2)}, u32[]{:S(2)}) async-start(bf16[16,2,1,2,16,256]{5,4,1,3,2,0:T(8,128)(2,1)} %copy.109), calls=%async_computation | async-start | bytes 1048576 | tf_op jit(solution)/shard_map/all_to_all | solution.py:133
  23.1 2.2 %copy-start.7 = (bf16[8,2,256]{2,1,0:T(2,128)(2,1)S(1)}, bf16[8,2,256]{2,1,0:T(2,128)(2,1)}, u32[]{:S(2)}) copy-start(bf16[8,2,256]{2,1,0:T(2,128)(2,1)} %param.17) | copy-start | bytes 24580
  23.2 2.3 %copy-start.13 = (s32[8]{0:T(128)S(1)}, s32[8]{0:T(128)}, u32[]{:S(2)}) copy-start(s32[8]{0:T(128)} %param.20) | copy-start | bytes 100
  23.2 2.4 %copy-start.11 = (bf16[8,4096]{1,0:T(8,128)(2,1)S(1)}, bf16[8,4096]{1,0:T(8,128)(2,1)}, u32[]{:S(2)}) copy-start(bf16[8,4096]{1,0:T(8,128)(2,1)} %param.16) | copy-start | bytes 196612
  25.7 2.1 %copy-start.3 = (bf16[8,256,2,128]{3,2,1,0:T(2,128)(2,1)S(1)}, bf16[8,256,2,128]{3,2,1,0:T(2,128)(2,1)}, u32[]{:S(2)}) copy-start(bf16[8,256,2,128]{3,2,1,0:T(2,128)(2,1)} %reshape_reshape_squeeze.15) | copy-start | bytes 3145732
  27.7 1.2 %copy-start.1 = (s32[16]{0:T(128)S(1)}, s32[16]{0:T(128)}, u32[]{:S(2)}) copy-start(s32[16]{0:T(128)} %param.23) | copy-start | bytes 196
  28.1 6.3 %copy-start.4 = (bf16[8,2,16,128]{3,2,1,0:T(8,128)(2,1)}, bf16[8,2,16,128]{3,2,1,0:T(8,128)(2,1)S(1)}, u32[]{:S(2)}) copy-start(bf16[8,2,16,128]{3,2,1,0:T(8,128)(2,1)S(1)} %fusion.7) | copy-start | bytes 196612
  28.9 5.4 %copy-start.10 = (bf16[1,2,32,128]{3,2,1,0:T(8,128)(2,1)}, bf16[1,2,32,128]{3,2,1,0:T(8,128)(2,1)S(1)}, u32[]{:S(2)}) copy-start(bf16[1,2,32,128]{3,2,1,0:T(8,128)(2,1)S(1)} %copy.142) | copy-start | bytes 49156
  35.1 6.4 %slice-start = ((bf16[8,2,16,128]{3,2,1,0:T(8,128)(2,1)}), bf16[2,2,16,128]{3,2,1,0:T(8,128)(2,1)S(1)}, s32[]{:S(2)}) async-start(bf16[8,2,16,128]{3,2,1,0:T(8,128)(2,1)} %copy-done.4), calls=%async_computation.1 | async-start | bytes 32768 | tf_op jit(solution)/shard_map/slice | solution.py:164
  35.1 6.5 %copy-start.5 = (bf16[8,4096]{1,0:T(8,128)(2,1)S(1)}, bf16[8,4096]{1,0:T(8,128)(2,1)}, u32[]{:S(2)}) copy-start(bf16[8,4096]{1,0:T(8,128)(2,1)} %param.15) | copy-start | bytes 196612
  36.9 4.6 %copy-start.12 = (pred[2]{0:T(512)(128)(4,1)S(1)}, pred[2]{0:T(512)(128)(4,1)}, u32[]{:S(2)}) copy-start(pred[2]{0:T(512)(128)(4,1)} %iota_compare_fusion.6) | copy-start | bytes 10
  36.9 4.9 %copy-start.8 = (f32[4096]{0:T(1024)S(1)}, f32[4096]{0:T(1024)}, u32[]{:S(2)}) copy-start(f32[4096]{0:T(1024)} %param.24) | copy-start | bytes 49156
  36.9 5.0 %copy-start.6 = (bf16[4096,8]{0,1:T(8,128)(2,1)S(1)}, bf16[4096,8]{0,1:T(8,128)(2,1)}, u32[]{:S(2)}) copy-start(bf16[4096,8]{0,1:T(8,128)(2,1)} %param.25) | copy-start | bytes 196612
  36.9 5.2 %copy-start.9 = (s32[8,8]{1,0:T(8,128)S(1)}, s32[8,8]{1,0:T(8,128)}, u32[]{:S(2)}) copy-start(s32[8,8]{1,0:T(8,128)} %param.29) | copy-start | bytes 772
  44.1 6.7 %collective-permute-start = (bf16[8,4224]{1,0:T(8,128)(2,1)S(1)}, bf16[8,4224]{1,0:T(8,128)(2,1)S(1)}, u32[]{:S(2)}, u32[]{:S(2)}) collective-permute-start(bf16[8,4224]{1,0:T(8,128)(2,1)S(1)} %get-tuple-element.11), channel_id=1, source_target_pairs={{0,8},{1,9},{2,10},{3,11},{4,12},{5,13},{6,14},{7,15},{8,0},{9,1},... | collective-permute-start | bytes 202760 | tf_op jit(solution)/shard_map/ppermute | solution.py:20
  50.9 5.1 %collective-permute-start.1 = (bf16[16,4224]{1,0:T(8,128)(2,1)S(1)}, bf16[16,4224]{1,0:T(8,128)(2,1)S(1)}, u32[]{:S(2)}, u32[]{:S(2)}) collective-permute-start(bf16[16,4224]{1,0:T(8,128)(2,1)S(1)} %pad_maximum_fusion.2), channel_id=1, source_target_pairs={{0,4},{1,5},{2,6},{3,7},{4,0},{5,1},{6,2},{7,3},{8,12},{9,13},{10,... | collective-permute-start | bytes 405512 | tf_op jit(solution)/shard_map/ppermute | solution.py:20
  56.0 10.3 %copy-start.2 = (bf16[1,4096,384]{2,1,0:T(8,128)(2,1)S(1)}, bf16[1,4096,384]{2,1,0:T(8,128)(2,1)}, u32[]{:S(2)}) copy-start(bf16[1,4096,384]{2,1,0:T(8,128)(2,1)} %param.27) | copy-start | bytes 9437188
  56.0 6.5 %collective-permute-start.2 = (bf16[32,4224]{1,0:T(8,128)(2,1)S(1)}, bf16[32,4224]{1,0:T(8,128)(2,1)S(1)}, u32[]{:S(2)}, u32[]{:S(2)}) collective-permute-start(bf16[32,4224]{1,0:T(8,128)(2,1)S(1)} %pad_maximum_fusion.1), channel_id=1, source_target_pairs={{0,2},{1,3},{2,0},{3,1},{4,6},{5,7},{6,4},{7,5},{8,10},{9,11},{10,... | collective-permute-start | bytes 811016 | tf_op jit(solution)/shard_map/ppermute | solution.py:20
  62.5 2.0 %collective-permute-start.3 = (bf16[64,4224]{1,0:T(8,128)(2,1)S(1)}, bf16[64,4224]{1,0:T(8,128)(2,1)S(1)}, u32[]{:S(2)}, u32[]{:S(2)}) collective-permute-start(bf16[64,4224]{1,0:T(8,128)(2,1)S(1)} %pad_maximum_fusion), channel_id=1, source_target_pairs={{0,1},{1,0},{2,3},{3,2},{4,5},{5,4},{6,7},{7,6},{8,9},{9,8},{10,11... | collective-permute-start | bytes 1622024 | tf_op jit(solution)/shard_map/ppermute | solution.py:20
  74.5 2.0 %collective-permute-start.4 = (bf16[64,4096]{1,0:T(8,128)(2,1)S(1)}, bf16[64,4096]{1,0:T(8,128)(2,1)S(1)}, u32[]{:S(2)}, u32[]{:S(2)}) collective-permute-start(bf16[64,4096]{1,0:T(8,128)(2,1)S(1)} %slice.146), channel_id=1, source_target_pairs={{0,1},{1,0},{2,3},{3,2},{4,5},{5,4},{6,7},{7,6},{8,9},{9,8},{10,11... | collective-permute-start | bytes 1572872 | tf_op jit(solution)/shard_map/ppermute | solution.py:20
  77.8 8.4 %collective-permute-start.5 = (bf16[32,4096]{1,0:T(8,128)(2,1)S(1)}, bf16[32,4096]{1,0:T(8,128)(2,1)S(1)}, u32[]{:S(2)}, u32[]{:S(2)}) collective-permute-start(bf16[32,4096]{1,0:T(8,128)(2,1)S(1)} %slice.147), channel_id=1, source_target_pairs={{0,2},{1,3},{2,0},{3,1},{4,6},{5,7},{6,4},{7,5},{8,10},{9,11},{10,... | collective-permute-start | bytes 786440 | tf_op jit(solution)/shard_map/ppermute | solution.py:20
  86.3 5.1 %collective-permute-start.6 = (bf16[16,4096]{1,0:T(8,128)(2,1)S(1)}, bf16[16,4096]{1,0:T(8,128)(2,1)S(1)}, u32[]{:S(2)}, u32[]{:S(2)}) collective-permute-start(bf16[16,4096]{1,0:T(8,128)(2,1)S(1)} %slice.148), channel_id=1, source_target_pairs={{0,4},{1,5},{2,6},{3,7},{4,0},{5,1},{6,2},{7,3},{8,12},{9,13},{10,... | collective-permute-start | bytes 393224 | tf_op jit(solution)/shard_map/ppermute | solution.py:20
  91.5 6.2 %collective-permute-start.7 = (bf16[8,4096]{1,0:T(8,128)(2,1)S(1)}, bf16[8,4096]{1,0:T(8,128)(2,1)S(1)}, u32[]{:S(2)}, u32[]{:S(2)}) collective-permute-start(bf16[8,4096]{1,0:T(8,128)(2,1)S(1)} %slice.149), channel_id=1, source_target_pairs={{0,8},{1,9},{2,10},{3,11},{4,12},{5,13},{6,14},{7,15},{8,0},{9,1},... | collective-permute-start | bytes 196616 | tf_op jit(solution)/shard_map/ppermute | solution.py:20
